TPU v7x, 256 devices: a whole 4x4x8 slice. The times are simulated.
256 devices in a mesh: dp: 32 (over y, z), mp: 8 (over x, core).
Axes of the slice: x: 4, y: 4, z: 8, core: 2. Of those that a mesh axis runs over, the one named last changes fastest.
Arguments:
- hidden_act: bfloat16 [8192, 14336], P('dp', 'mp'), may hold values from -6 to 6
- readout: bfloat16 [8192, 2560], P('dp'), may hold values from -6 to 6
- log_gap: float32 [1024, 8], P('dp'), may hold values from -0.6 to 0.6
- advantage: float32 [1024], P('dp'), may hold values from -6 to 6
- version: int32 [1024], P('dp'), may hold values from 0 to 3
- lengths: int32 [32, 32], P('dp'), may hold values from 1 to 8, 224 in all within a row
- routes: int32 [1024, 1], P('dp'), may hold values from 0 to 31; in each aligned block of 32 rows (0 to 31, 32 to 63, ...) at most 2 rows name the same one
- weight: bfloat16 [14336, 2560], P(('mp', 'dp')), may hold values from -0.046875 to 0.046875
Outputs:
- log_ratio: float32 [2048, 8], P('dp')
- weight_grad: float32 [14336, 2560], P(('mp', 'dp'))
Inputs may be any that keep to these rules, and one draw needn't show every extreme that they name: `routes`: among the 32 responses of one generator device at most 2 name the same learner shard, and some shard receives exactly 2; every learner shard receives at least one response. The lengths of one generator device's responses sum to 224, and one of them is 8.
All inputs are finite; a program needn't handle non-finite values.
Results may differ from a plain program's by a relative error of at most 0.0029.
Values may be sent and summed in bfloat16 or wider, within the bound.
A program may use at most 64 MiB of HBM per device.

v0:
```python
import math

import jax
import jax.numpy as jnp
from jax import lax
from jax.sharding import PartitionSpec as P

NVER = 4


def token_shift(rows_act, rows_read, weight):
    width = rows_read.shape[1]
    layer_out = jnp.dot(
        rows_act,
        lax.all_gather(weight, "dp", axis=0, tiled=True),
        preferred_element_type=jnp.float32,
    )
    partial_dot = jnp.sum(layer_out * rows_read.astype(jnp.float32), axis=1)
    return lax.psum(partial_dot, "mp") * (0.15 / math.sqrt(width))


def surrogate_coef(logit_all, live, stale, adv, count_each):
    ratio = jnp.exp(logit_all)
    squash = jnp.tanh((ratio - 1.0) / 0.2)
    clipped = 1.0 + 0.2 * squash
    adv_col = adv[:, None]
    plain = ratio * adv_col <= clipped * adv_col
    slope = jnp.where(plain, 1.0, 1.0 - squash * squash)
    return jnp.where(
        live, -512.0 * stale[:, None] * adv_col * ratio * slope / count_each[:, None], 0.0
    )


def weight_terms(rows_act, out_grad):
    full_term = lax.dot_general(
        rows_act, out_grad, (((0,), (0,)), ((), ())), preferred_element_type=jnp.float32
    )
    return lax.psum_scatter(full_term, "dp", scatter_dimension=0, tiled=True)


def body(hidden_act, readout, log_gap, advantage, version, lengths, routes, weight):
    shards = lax.axis_size("dp")
    respond, seglen = log_gap.shape
    width = readout.shape[1]
    hidden_local = hidden_act.shape[1]
    slots = 2 * respond // shards
    total_slots = shards * slots
    dest = routes[:, 0]
    onehot = (dest[:, None] == jnp.arange(shards, dtype=jnp.int32)[None, :]).astype(jnp.int32)
    rank = jnp.sum((jnp.cumsum(onehot, axis=0) - onehot) * onehot, axis=1)
    slot_of = dest * slots + rank
    select = (jnp.arange(total_slots, dtype=jnp.int32)[:, None] == slot_of[None, :]).astype(
        jnp.float32
    )
    lens = lengths[0]
    lens_float = lens.astype(jnp.float32)
    stale = jnp.power(jnp.float32(0.7), (NVER - 1 - version).astype(jnp.float32))
    positions = jnp.arange(seglen, dtype=jnp.int32)
    scale_out = 0.15 / math.sqrt(width)
    select_bf = select.astype(jnp.bfloat16)
    send_act = jnp.dot(
        select_bf,
        hidden_act.reshape(respond, seglen * hidden_local),
        preferred_element_type=jnp.float32,
    ).astype(jnp.bfloat16)
    send_read = jnp.dot(
        select_bf, readout.reshape(respond, seglen * width), preferred_element_type=jnp.float32
    ).astype(jnp.bfloat16)
    highest = lax.Precision.HIGHEST
    send_gap = jnp.dot(select, log_gap, precision=highest)
    send_adv = jnp.dot(select, advantage, precision=highest)
    send_stale = jnp.dot(select, stale, precision=highest)
    send_len = jnp.dot(select, lens_float, precision=highest)
    recv_act, recv_read = (
        lax.all_to_all(send_act, "dp", split_axis=0, concat_axis=0, tiled=True),
        lax.all_to_all(send_read, "dp", split_axis=0, concat_axis=0, tiled=True),
    )
    recv_gap, recv_adv, recv_stale, recv_len = (
        lax.all_to_all(send_gap, "dp", split_axis=0, concat_axis=0, tiled=True),
        lax.all_to_all(send_adv, "dp", split_axis=0, concat_axis=0, tiled=True),
        lax.all_to_all(send_stale, "dp", split_axis=0, concat_axis=0, tiled=True),
        lax.all_to_all(send_len, "dp", split_axis=0, concat_axis=0, tiled=True),
    )
    rows_act = recv_act.reshape(total_slots * seglen, hidden_local)
    rows_read = recv_read.reshape(total_slots * seglen, width)
    shift = token_shift(rows_act, rows_read, weight)
    logit_all = recv_gap + shift.reshape(total_slots, seglen)
    live = positions[None, :].astype(jnp.float32) < recv_len[:, None]
    log_ratio = jnp.where(live, logit_all, 0.0)
    count_here = jnp.sum(recv_len)
    count_each = jnp.broadcast_to(count_here, recv_len.shape)
    coef = surrogate_coef(logit_all, live, recv_stale, recv_adv, count_each)
    out_grad = (coef.reshape(-1)[:, None] * scale_out * rows_read.astype(jnp.float32)).astype(
        jnp.bfloat16
    )
    weight_grad = weight_terms(rows_act, out_grad)
    return (log_ratio, weight_grad)


def solution(mesh):
    placed = (
        P("dp", "mp"),
        P("dp", None),
        P("dp", None),
        P("dp"),
        P("dp"),
        P("dp", None),
        P("dp", None),
        P(("mp", "dp"), None),
    )
    return jax.shard_map(
        body,
        mesh=mesh,
        in_specs=placed,
        out_specs=(P("dp", None), P(("mp", "dp"), None)),
        check_vma=False,
    )
```

profile of v0, /device:TPU:1, one launch (start us, length us, event | category | flops | bytes accessed | tf_op | source)
XLA Modules:
  0.0 520.8 jit_solution(5700732834719712697)
XLA Ops:
  7.2 0.7 all-gather.2.cloned.1.call-update
  7.9 0.7 fusion.8
  8.7 0.8 select_reduce_fusion
  9.5 0.7 multiply_add_fusion.1
  10.2 0.8 convolution_bitcast_fusion.1
  11.0 0.7 all_to_all.48
  11.7 12.0 %all-to-all-start.4 = ((f32[32,2,1]{1,2,0:T(1,128)}), f32[32,2,1]{1,2,0:T(1,128)S(1)}, u32[]{:S(2)}, u32[]{:S(2)}) async-start(f32[32,2,1]{1,2,0:T(1,128)} %bitcast.9), calls=%async_computation.4 | async-start | bytes 32768 | tf_op jit(solution)/shard_map/all_to_all | solution.py:81
  23.8 0.1 broadcast_compare_fusion
  23.9 0.8 convolution_bitcast_fusion
  24.6 0.8 all_to_all.50
  25.4 7.0 %all-to-all-done.4 = f32[32,2,1]{1,2,0:T(1,128)S(1)} async-done(((f32[32,2,1]{1,2,0:T(1,128)}), f32[32,2,1]{1,2,0:T(1,128)S(1)}, u32[]{:S(2)}, u32[]{:S(2)}) %all-to-all-start.4) | async-done | bytes 288 | tf_op jit(solution)/shard_map/all_to_all | solution.py:81
  32.4 3.8 all-to-all-start.5
  36.2 0.8 fusion.1
  37.0 0.8 copy.14
  37.8 7.2 %all-to-all-done.5 = f32[32,2,1]{1,2,0:T(1,128)S(1)} async-done(((f32[32,2,1]{1,2,0:T(1,128)}), f32[32,2,1]{1,2,0:T(1,128)S(1)}, u32[]{:S(2)}, u32[]{:S(2)}) %all-to-all-start.5) | async-done | bytes 288 | tf_op jit(solution)/shard_map/all_to_all | solution.py:80
  45.0 3.8 all-to-all-start
  48.8 0.8 fusion
  49.6 1.6 reshape.111
  51.1 6.4 %all-to-all-done = f32[32,2,1]{1,2,0:T(1,128)S(1)} async-done(((f32[32,2,1]{1,2,0:T(1,128)}), f32[32,2,1]{1,2,0:T(1,128)S(1)}, u32[]{:S(2)}, u32[]{:S(2)}) %all-to-all-start) | async-done | bytes 288 | tf_op jit(solution)/shard_map/all_to_all | solution.py:82
  57.5 3.9 all-to-all-start.1
  61.4 0.6 convolution_convert_fusion.1
  62.0 2.1 all_to_all.44
  64.1 6.1 %all-to-all-done.1 = f32[32,2,8]{2,1,0:T(2,128)S(1)} async-done(((f32[32,2,8]{2,1,0:T(2,128)}), f32[32,2,8]{2,1,0:T(2,128)S(1)}, u32[]{:S(2)}, u32[]{:S(2)}) %all-to-all-start.1) | async-done | bytes 2080 | tf_op jit(solution)/shard_map/all_to_all | solution.py:79
  70.2 4.7 all-to-all-start.2
  74.9 1.5 reshape.113
  76.4 2.1 convolution_convert_fusion
  78.5 3.0 all_to_all.46
  81.5 50.8 %all-to-all-done.2 = bf16[32,2,14336]{2,1,0:T(2,128)(2,1)} async-done(((bf16[32,2,14336]{2,1,0:T(2,128)(2,1)}), bf16[32,2,14336]{2,1,0:T(2,128)(2,1)}, u32[]{:S(2)}, u32[]{:S(2)}) %all-to-all-start.2) | async-done | bytes 1835040 | tf_op jit(solution)/shard_map/all_to_all | solution.py:75
  132.3 10.8 %all-to-all-start.3 = ((bf16[32,2,20480]{2,1,0:T(2,128)(2,1)}), bf16[32,2,20480]{2,1,0:T(2,128)(2,1)S(1)}, u32[]{:S(2)}, u32[]{:S(2)}) async-start(bf16[32,2,20480]{2,1,0:T(2,128)(2,1)} %all_to_all.46), calls=%async_computation.3 | async-start | bytes 5242880 | tf_op jit(solution)/shard_map/all_to_all | solution.py:76
  143.3 0.5 broadcast.73
  143.8 0.7 reduce.12
  144.6 1.3 fusion.17
  146.1 0.1 lt.23
  146.5 0.1 all_to_all.53
  146.6 5.3 %reshape.112 = bf16[512,1792]{1,0:T(8,128)(2,1)} reshape(bf16[32,2,14336]{2,1,0:T(2,128)(2,1)} %all-to-all-done.2) | data formatting | bytes 3670016 | tf_op jit(solution)/shard_map/reshape | solution.py:84
  152.0 54.5 %all-to-all-done.3 = bf16[32,2,20480]{2,1,0:T(2,128)(2,1)S(1)} async-done(((bf16[32,2,20480]{2,1,0:T(2,128)(2,1)}), bf16[32,2,20480]{2,1,0:T(2,128)(2,1)S(1)}, u32[]{:S(2)}, u32[]{:S(2)}) %all-to-all-start.3) | async-done | bytes 2621472 | tf_op jit(solution)/shard_map/all_to_all | solution.py:76
  206.5 3.3 reshape.115
  209.8 10.6 %multiply_reduce_fusion = f32[512]{0:T(512)S(1)} fusion(f32[512,2560]{1,0:T(8,128)} %reshape.115, bf16[512,1792]{1,0:T(8,128)(2,1)} %reshape.112, bf16[1792,2560]{1,0:T(8,128)(2,1)} %all-gather.2.cloned.1.call-done), kind=kOutput, calls=%fused_computation.3 | convolution fusion | flops 4700241408 | bytes 16254976 | tf_op jit(solution)/shard_map/dot_general | solution.py:13
  220.4 17.4 %psum.7 = f32[512]{0:T(512)S(1)} all-reduce(f32[512]{0:T(512)S(1)} %multiply_reduce_fusion), channel_id=1, replica_groups=mesh['dp'=32,'mp'=8] {'mp'}, use_global_device_ids=true, to_apply=%region_3.4 | all-reduce | flops 512 | bytes 4096 | tf_op jit(solution)/shard_map/psum | solution.py:19
  237.8 0.7 fusion.9
  238.5 0.1 mul.128
  238.6 2.8 mul.129
  241.4 8.5 %mul.130 = f32[32,2,20480]{2,1,0:T(2,128)} reshape(f32[32,2,8,2560]{3,2,1,0:T(8,128)} %mul.129) | data formatting | bytes 10485760 | tf_op jit(solution)/shard_map/mul | solution.py:93
  249.9 7.0 %multiply_convert_fusion = bf16[32,2,20480]{2,1,0:T(2,128)(2,1)} fusion(f32[32,2,20480]{2,1,0:T(2,128)} %mul.130, bf16[32,2,20480]{2,1,0:T(2,128)(2,1)S(1)} %all-to-all-done.3), kind=kLoop, calls=%fused_computation.2 | loop fusion | flops 3932160 | bytes 10485760 | tf_op jit(solution)/shard_map/convert_element_type | solution.py:93
  256.9 6.6 %convert_element_type.66 = bf16[512,2560]{1,0:T(8,128)(2,1)S(1)} reshape(bf16[32,2,20480]{2,1,0:T(2,128)(2,1)} %multiply_convert_fusion) | data formatting | bytes 5242880 | tf_op jit(solution)/shard_map/convert_element_type | solution.py:93
  263.5 10.6 %fusion.18 = f32[1792,2560]{1,0:T(8,128)} fusion(bf16[512,1792]{1,0:T(8,128)(2,1)} %reshape.112, bf16[512,2560]{1,0:T(8,128)(2,1)S(1)} %convert_element_type.66), kind=kOutput, calls=%fused_computation.40 | convolution fusion | flops 4697620480 | bytes 22806528 | tf_op jit(solution)/shard_map/dot_general | solution.py:35
  274.2 0.7 copy.18
  274.9 239.1 %reduce-scatter.2.cloned.1.call-done = f32[56,2560]{1,0:T(8,128)} async-done(((f32[1792,2560]{1,0:T(8,128)}), f32[56,2560]{1,0:T(8,128)}) %reduce-scatter.2.cloned.1.call-update) | async-done | bytes 573456 | tf_op jit(solution)/shard_map/reduce_scatter | solution.py:38
  (25 shorter events, 1.1 us)
Async XLA Ops:
  7.2 41.6 %copy-start = (f32[32,8]{0,1:T(8,128)S(1)}, f32[32,8]{0,1:T(8,128)}, u32[]{:S(2)}) copy-start(f32[32,8]{0,1:T(8,128)} %param.10) | copy-start | bytes 3076
  7.2 202.6 %all-gather.2.cloned.1.call-start = ((), (), s32[]{:S(2)}) async-start(), calls=%async_computation.7 | async-start | bytes 9461760 | tf_op jit(solution)/shard_map/all_gather | solution.py:15
  11.7 20.7 %all-to-all-start.4 = ((f32[32,2,1]{1,2,0:T(1,128)}), f32[32,2,1]{1,2,0:T(1,128)S(1)}, u32[]{:S(2)}, u32[]{:S(2)}) async-start(f32[32,2,1]{1,2,0:T(1,128)} %bitcast.9), calls=%async_computation.4 | async-start | bytes 32768 | tf_op jit(solution)/shard_map/all_to_all | solution.py:81
  32.4 12.6 %all-to-all-start.5 = ((f32[32,2,1]{1,2,0:T(1,128)}), f32[32,2,1]{1,2,0:T(1,128)S(1)}, u32[]{:S(2)}, u32[]{:S(2)}) async-start(f32[32,2,1]{1,2,0:T(1,128)} %bitcast.12), calls=%async_computation.5 | async-start | bytes 32768 | tf_op jit(solution)/shard_map/all_to_all | solution.py:80
  45.0 12.5 %all-to-all-start = ((f32[32,2,1]{1,2,0:T(1,128)}), f32[32,2,1]{1,2,0:T(1,128)S(1)}, u32[]{:S(2)}, u32[]{:S(2)}) async-start(f32[32,2,1]{1,2,0:T(1,128)} %copy.14), calls=%async_computation | async-start | bytes 32768 | tf_op jit(solution)/shard_map/all_to_all | solution.py:82
  57.5 12.7 %all-to-all-start.1 = ((f32[32,2,8]{2,1,0:T(2,128)}), f32[32,2,8]{2,1,0:T(2,128)S(1)}, u32[]{:S(2)}, u32[]{:S(2)}) async-start(f32[32,2,8]{2,1,0:T(2,128)} %bitcast.5), calls=%async_computation.1 | async-start | bytes 65536 | tf_op jit(solution)/shard_map/all_to_all | solution.py:79
  64.1 10.8 %copy-start.2 = (bf16[256,2560]{1,0:T(8,128)(2,1)S(1)}, bf16[256,2560]{1,0:T(8,128)(2,1)}, u32[]{:S(2)}) copy-start(bf16[256,2560]{1,0:T(8,128)(2,1)} %param.9) | copy-start | bytes 3932164
  70.2 62.1 %all-to-all-start.2 = ((bf16[32,2,14336]{2,1,0:T(2,128)(2,1)}), bf16[32,2,14336]{2,1,0:T(2,128)(2,1)}, u32[]{:S(2)}, u32[]{:S(2)}) async-start(bf16[32,2,14336]{2,1,0:T(2,128)(2,1)} %all_to_all.44), calls=%async_computation.2 | async-start | bytes 3670016 | tf_op jit(solution)/shard_map/all_to_all | solution.py:75
  132.3 74.2 %all-to-all-start.3 = ((bf16[32,2,20480]{2,1,0:T(2,128)(2,1)}), bf16[32,2,20480]{2,1,0:T(2,128)(2,1)S(1)}, u32[]{:S(2)}, u32[]{:S(2)}) async-start(bf16[32,2,20480]{2,1,0:T(2,128)(2,1)} %all_to_all.46), calls=%async_computation.3 | async-start | bytes 5242880 | tf_op jit(solution)/shard_map/all_to_all | solution.py:76
  143.0 370.9 %reduce-scatter.2.cloned.1.call-start = ((), (), s32[]{:S(2)}) async-start(), calls=%async_computation.8 | async-start | bytes 18923520 | tf_op jit(solution)/shard_map/reduce_scatter | solution.py:38
  274.0 239.9 %copy-start.1 = (f32[32,8]{0,1:T(8,128)S(1)}, f32[32,8]{0,1:T(8,128)}, u32[]{:S(2)}) copy-start(f32[32,8]{0,1:T(8,128)} %param.10) | copy-start | bytes 3076
Sparse Core Ops, SparseCore 0:
  10.6 149.5 all-gather.1
  274.2 239.7 reduce-scatter.1
where the time goes:
time: 525 us; the launch traced here: 521 us
  waiting for transfers between devices  372 us (71%)
  local copies, waits for them, and re-layouts  39.1 us (7%)
  starting transfers between devices  39.1 us (7%)
  matrix products  27 us (5%)
  blocking collectives  17.4 us (3%)
  between operations  14.2 us (3%)
  other arithmetic  12.3 us (2%)
    reduce_scatter x1, waiting for transfers between devices, weight_terms(): return lax.psum_scatter(full_term, 'dp', scatter_dimension=0, tiled=True)  239 us
    all_to_all x1, waiting for transfers between devices, body(): lax.all_to_all(send_read, 'dp', split_axis=0, concat_axis=0, tiled=True)  54.5 us
    all_to_all x1, waiting for transfers between devices, body(): lax.all_to_all(send_act, 'dp', split_axis=0, concat_axis=0, tiled=True)  50.8 us
    psum x1, blocking collectives, token_shift(): return lax.psum(partial_dot, 'mp') * (0.15 / math.sqrt(width))  17.4 us
    all_to_all x1, starting transfers between devices, body(): lax.all_to_all(send_stale, 'dp', split_axis=0, concat_axis=0, tiled=True)  12 us
    mul x3, local copies, waits for them, and re-layouts, body(): coef.reshape(-1)[:, None] * scale_out * rows_read.astype(jnp.float32)  11.4 us
    all_to_all x1, starting transfers between devices, body(): lax.all_to_all(send_read, 'dp', split_axis=0, concat_axis=0, tiled=True)  10.8 us
    dot_general x1, matrix products, token_shift(): jnp.dot(rows_act, lax.all_gather(weight, 'dp', axis=0, tiled=True), prefe...  10.6 us
  transfers between devices with their start and end apart: 8, of which 7 were waited for; matrix products, arithmetic and copies ran while one was open for 5% of the time, Pallas kernels for 0%

commit v1 on v0

v1 whole, which is shorter than its diff:
```python
import functools
import math

import jax
import jax.numpy as jnp
from jax import lax
from jax.experimental import pallas as pl
from jax.experimental.pallas import tpu as pltpu
from jax.sharding import PartitionSpec as P

MESH = pl.DeviceIdType.MESH
BF = jnp.bfloat16
F32 = jnp.float32

NX, NY, NZ = 4, 4, 8
TOK = 256
DH = 1280
ROWS = 56
FB = ROWS * NZ
FALL = 2 * FB
CH = 256
NCH = DH // CH
NSEM = 140


def hdot(a, b):
    return lax.dot_general(
        a, b, (((1,), (0,)), ((), ())), precision=lax.Precision.HIGHEST,
        preferred_element_type=F32,
    )


def iota(shape, dim):
    return lax.broadcasted_iota(jnp.int32, shape, dim)


def kernel(scale_out, h_in, r_in, w_in, gap_ref, adv_ref, ver_ref, len_ref, route_ref,
           lr_out, g_out,
           wbuf, wcat, rbuf, hv, htr, ht, relay, pkf, kb, ar1, ar2, lb, og, gbuf,
           rss, rsr, stage, local_sem, send_sem, recv_sem):
    dp = lax.axis_index("dp")
    mp = lax.axis_index("mp")
    y, z = dp // NZ, dp % NZ
    x, c = mp // 2, mp % 2
    px = x % 2
    o = 1 - c
    yp, ym, y2 = (y + 1) % NY, (y + 3) % NY, (y + 2) % NY
    zp, zm = (z + 1) % NZ, (z + 7) % NZ
    xp, xm = (x + 1) % NX, (x + 3) % NX

    def dev(yy, zz, xx, cc):
        return (yy * NZ + zz, xx * 2 + cc)

    d_yp, d_ym, d_y2 = dev(yp, z, x, c), dev(ym, z, x, c), dev(y2, z, x, c)
    d_zp, d_zm = dev(y, zp, x, c), dev(y, zm, x, c)
    d_xp, d_xm = dev(y, z, xp, c), dev(y, z, xm, c)
    d_co = dev(y, z, x, o)

    count = [0]
    sent = []

    def send(src, dst, where):
        n = count[0]
        count[0] += 1
        copy = pltpu.make_async_remote_copy(
            src_ref=src, dst_ref=dst, send_sem=send_sem.at[n], recv_sem=recv_sem.at[n],
            device_id=where, device_id_type=MESH,
        )
        copy.start()
        sent.append(copy)
        return copy

    half = pl.ds(pl.multiple_of(c * DH, 128), DH)
    other = pl.ds(pl.multiple_of(o * DH, 128), DH)
    mine = pl.ds(pl.multiple_of(y * TOK, TOK), TOK)
    cp_h = pltpu.make_async_copy(h_in, hv, local_sem.at[0])
    cp_h.start()
    cp_r = pltpu.make_async_copy(r_in.at[:, half], rbuf.at[mine, :], local_sem.at[1])
    cp_r.start()
    cp_w = pltpu.make_async_copy(w_in.at[:, half], wbuf.at[c, z], local_sem.at[2])
    cp_w.start()

    barrier = pltpu.get_barrier_semaphore()
    greet = [d_zp, d_zm, d_yp, d_ym, d_y2]
    greet += [(dp, (mp + k) % 8) for k in range(1, 8)]
    for where in greet:
        pl.semaphore_signal(barrier, inc=1, device_id=where, device_id_type=MESH)
    pl.semaphore_wait(barrier, len(greet))

    W = {}
    w_own = w_in.at[:, half]
    w_co = send(w_in.at[:, other], wbuf.at[c, z], d_co)
    W[0, 0, 1] = send(w_own, wbuf.at[c, z], d_zp)
    W[0, 1, 1] = send(w_own, wbuf.at[c, z], d_zm)

    hb = px * 128

    def rows_in(part):
        return pl.ds(pl.multiple_of(hb + part * 64, 64), 64)

    def rows_at(yy, part):
        return pl.ds(pl.multiple_of(yy * TOK + hb + part * 64, 64), 64)

    def r_first(part, where):
        return send(r_in.at[rows_in(part), half], rbuf.at[rows_at(y, part), :], where)

    rp_a = r_first(0, d_yp)
    rm_b = r_first(1, d_ym)
    rp_b = r_first(1, d_yp)
    rm_a = r_first(0, d_ym)

    cp_h.wait()
    for j in range(7):
        htr[j * 256:(j + 1) * 256, :] = hv[:, j * 256:(j + 1) * 256].T

    def h_rows(yy, first, rows):
        return pl.ds(pl.multiple_of(yy * FB + first, 32), rows)

    def cols_at(yy):
        return pl.ds(pl.multiple_of(yy * TOK, TOK), TOK)

    h2p = send(htr.at[h_rows(y2, 0, FB // 2), :], relay.at[0], d_yp)
    h2m = send(htr.at[h_rows(y2, FB // 2, FB // 2), :], relay.at[1], d_ym)

    w_co.wait_recv()
    W[1, 0, 1] = send(wbuf.at[o, z], wbuf.at[o, z], d_zp)
    W[1, 1, 1] = send(wbuf.at[o, z], wbuf.at[o, z], d_zm)

    cp_ho = pltpu.make_async_copy(
        htr.at[h_rows(y, 0, FB), :], ht.at[c, :, cols_at(y)], local_sem.at[3])
    cp_ho.start()

    dest_b = jnp.broadcast_to(route_ref[...].astype(F32), (32, 32))
    ri, ci = iota((32, 32), 0), iota((32, 32), 1)
    dest_row = jnp.sum(jnp.where(ri == ci, dest_b, 0.0), axis=0, keepdims=True)
    earlier = jnp.where((dest_b == dest_row) & (ri < ci), 1.0, 0.0)
    rank_row = jnp.sum(earlier, axis=0, keepdims=True)
    key_row = dest_row * 2.0 + rank_row
    ver = ver_ref[...]
    stale_row = jnp.where(
        ver == 3, 1.0, jnp.where(ver == 2, 0.7, jnp.where(ver == 1, 0.7 ** 2, 0.7 ** 3))
    ).astype(F32)
    row8, resp8 = iota((8, 32), 0), iota((8, 32), 1)
    mine8 = (row8 // 2 == y) & (resp8 // 16 == row8 % 2)
    spread = jnp.where(iota((32, 128), 0) % 16 == iota((32, 128), 1) // 8, 1.0, 0.0)

    def lay(v):
        return hdot(jnp.where(mine8, jnp.broadcast_to(v, (8, 32)), 0.0), spread)

    tile = jnp.where(iota((8, 128), 0) == iota((8, 128), 1) % 8, 1.0, 0.0)
    gap_wide = hdot(gap_ref[...], tile) * spread
    own_rows = iota((8, 128), 0) // 2 == y
    position = (iota((8, 128), 1) % 8).astype(F32)
    len_t = lay(len_ref[...].astype(F32))
    pkf[y, 0] = hdot(jnp.where(mine8, 1.0, 0.0), gap_wide)
    pkf[y, 1] = jnp.where(own_rows & (position >= len_t), -1.0, lay(key_row))
    pkf[y, 2] = lay(adv_ref[...])
    pkf[y, 3] = lay(stale_row)
    pk = [send(pkf.at[y], pkf.at[y], d) for d in (d_yp, d_ym, d_y2)]

    def w_forward(k, s):
        core = c if k == 0 else o
        for d, where in ((0, d_zp), (1, d_zm)):
            W[k, d, s].wait_recv()
            origin = (z + (8 - s if d == 0 else s)) % NZ
            if s < 3:
                ref = wbuf.at[core, origin]
            else:
                ref = wbuf.at[core, origin, :, d * (DH // 2):(d + 1) * (DH // 2)]
            W[k, d, s + 1] = send(ref, ref, where)

    w_forward(0, 1)

    def along(ref_rows, where):
        ref = rbuf.at[ref_rows, :]
        return send(ref, ref, where)

    rp_a.wait_recv()
    r2a = along(rows_at(ym, 0), d_yp)
    xa = [along(rows_at(ym, 0), d_xm)]
    rm_b.wait_recv()
    r2b = along(rows_at(yp, 1), d_ym)
    xb = [along(rows_at(yp, 1), d_xp)]

    h1p = send(htr.at[h_rows(yp, 0, FB), :], ht.at[c, :, cols_at(y)], d_yp)
    h1m = send(htr.at[h_rows(ym, 0, FB), :], ht.at[c, :, cols_at(y)], d_ym)
    cp_ho.wait()
    hp = [send(ht.at[c, :, cols_at(y)], ht.at[c, :, cols_at(y)], d_co)]

    w_forward(1, 1)

    rp_b.wait_recv()
    xb.append(along(rows_at(ym, 1), d_xp))
    rm_a.wait_recv()
    xa.append(along(rows_at(yp, 0), d_xm))

    for copy in pk:
        copy.wait_recv()
    fields = [pkf[0, f] + pkf[1, f] + pkf[2, f] + pkf[3, f] for f in range(4)]
    kb[z] = fields[1]
    K = {}
    K[0, 1] = send(kb.at[z], kb.at[z], d_zp)
    K[1, 1] = send(kb.at[z], kb.at[z], d_zm)

    def ring_forward(table, buf, s):
        for d, where in ((0, d_zp), (1, d_zm)):
            if (d, s) not in table:
                continue
            table[d, s].wait_recv()
            if s + 1 > (4 if d == 0 else 3):
                continue
            origin = (z + (8 - s if d == 0 else s)) % NZ
            table[d, s + 1] = send(buf.at[origin], buf.at[origin], where)

    w_forward(0, 2)

    h2p.wait_recv()
    hq_p = send(relay.at[0], ht.at[c, 0:FB // 2, cols_at(ym)], d_yp)
    h2m.wait_recv()
    hq_m = send(relay.at[1], ht.at[c, FB // 2:FB, cols_at(yp)], d_ym)

    w_forward(1, 2)
    ring_forward(K, kb, 1)

    r2a.wait_recv()
    xa.append(along(rows_at(y2, 0), d_xm))
    r2b.wait_recv()
    xb.append(along(rows_at(y2, 1), d_xp))

    w_forward(0, 3)

    h1p.wait_recv()
    hp.append(send(ht.at[c, :, cols_at(ym)], ht.at[c, :, cols_at(ym)], d_co))
    h1m.wait_recv()
    hp.append(send(ht.at[c, :, cols_at(yp)], ht.at[c, :, cols_at(yp)], d_co))

    w_forward(1, 3)
    ring_forward(K, kb, 2)

    hq_p.wait_recv()
    hq_m.wait_recv()
    hp.append(send(ht.at[c, :, cols_at(y2)], ht.at[c, :, cols_at(y2)], d_co))

    cp_r.wait()
    cp_w.wait()
    for copy in xa + xb:
        copy.wait_recv()
    for k in range(2):
        for d in range(2):
            W[k, d, 4].wait_recv()
    ring_forward(K, kb, 3)
    for copy in hp:
        copy.wait_recv()

    for core in range(2):
        for j in range(NZ // 2):
            for n in range(NCH):
                cols = slice(n * CH, (n + 1) * CH)
                pair = jnp.concatenate(
                    [wbuf[core, 2 * j, :, cols].astype(F32),
                     wbuf[core, 2 * j + 1, :, cols].astype(F32)], axis=0)
                first = core * FB + 2 * j * ROWS
                wcat[first:first + 2 * ROWS, cols] = pair.astype(BF)
    parts = []
    for b in range(NY):
        u = lax.dot_general(
            wcat[...], rbuf[b * TOK:(b + 1) * TOK, :], (((1,), (1,)), ((), ())),
            preferred_element_type=F32,
        )
        h = ht[:, :, b * TOK:(b + 1) * TOK].reshape(FALL, TOK).astype(F32)
        s = jnp.sum(u * h, axis=0, keepdims=True)
        parts += [s[:, 0:128], s[:, 128:256]]
    ar1[mp] = jnp.concatenate(parts, axis=0)
    first_stage = [
        send(ar1.at[mp], ar1.at[mp], (dp, (mp + k) % 8)) for k in range(1, 8)
    ]
    ring_forward(K, kb, 4)

    keys = [jnp.floor(kb[i] * 0.5) for i in range(NZ)]
    own_dest = jnp.floor(fields[1] * 0.5)
    count_each = jnp.ones((8, 128), F32)
    for k in range(NY * NZ):
        hits = jnp.zeros((8, 128), F32)
        for i in range(NZ):
            hits = hits + jnp.where(keys[i] == float(k), 1.0, 0.0)
        total = jnp.sum(jnp.sum(hits, axis=0, keepdims=True), axis=1, keepdims=True)
        count_each = jnp.where(own_dest == float(k), jnp.broadcast_to(total, (8, 128)), count_each)

    for copy in first_stage:
        copy.wait_recv()
    acc = ar1[0]
    for i in range(1, 8):
        acc = acc + ar1[i]
    ar2[y] = acc
    second_stage = [send(ar2.at[y], ar2.at[y], d) for d in (d_yp, d_ym, d_y2)]
    for copy in second_stage:
        copy.wait_recv()
    total = (ar2[0] + ar2[1]) + (ar2[2] + ar2[3])

    gap, key, adv, stale = fields
    live = key >= 0.0
    logit = gap + total * scale_out
    lb[z] = jnp.where(live, logit, 0.0)
    ratio = jnp.exp(logit)
    squash = jnp.tanh((ratio - 1.0) / 0.2)
    clipped = 1.0 + 0.2 * squash
    plain = ratio * adv <= clipped * adv
    slope = jnp.where(plain, 1.0, 1.0 - squash * squash)
    coef = jnp.where(live, -512.0 * stale * adv * ratio * slope / count_each, 0.0)
    coef_col = (coef * scale_out).T

    RS = {}

    def push(d, s, n, cols, where):
        RS[d, s, n] = send(rss.at[d, s - 1, n, :, :, cols], rsr.at[d, s - 1, n, :, :, cols], where)

    ends = ((0, d_zp), (1, d_zm))
    sides = (slice(0, CH // 2), slice(CH // 2, CH))
    far = (z + 4) % NZ
    hall = ht[...].reshape(FALL, NY * TOK)
    for n in range(NCH):
        cols = slice(n * CH, (n + 1) * CH)
        for b in range(8):
            rows = slice(b * 128, (b + 1) * 128)
            og[rows, cols] = (coef_col[:, b:b + 1] * rbuf[rows, cols].astype(F32)).astype(BF)
        g = jnp.dot(hall, og[:, cols], preferred_element_type=F32)
        gbuf[n] = g.reshape(2, NZ, ROWS, CH)
        for d, where in ends:
            rss[d, 0, n, :, :, sides[d]] = gbuf[n, :, far, :, sides[d]].astype(BF)
            push(d, 1, n, sides[d], where)

    L = {}
    L[0, 1] = send(lb.at[z], lb.at[z], d_zp)
    L[1, 1] = send(lb.at[z], lb.at[z], d_zm)

    full = slice(0, CH)
    for s in range(2, 5):
        for n in range(NCH):
            for d, where in ends:
                to = (z + (5 - s if d == 0 else 3 + s)) % NZ
                RS[d, s - 1, n].wait_recv()
                if s == 2:
                    a, b = sides[d], sides[1 - d]
                    rss[d, 1, n, :, :, a] = (
                        gbuf[n, :, to, :, a] + rsr[d, 0, n, :, :, a].astype(F32)).astype(BF)
                    rss[d, 1, n, :, :, b] = gbuf[n, :, to, :, b].astype(BF)
                else:
                    rss[d, s - 1, n] = (
                        gbuf[n, :, to] + rsr[d, s - 2, n].astype(F32)).astype(BF)
                push(d, s, n, full, where)
        ring_forward(L, lb, s - 1)

    last = []
    for n in range(NCH):
        for d, _ in ends:
            RS[d, 4, n].wait_recv()
        cols = pl.ds(pl.multiple_of(c * DH + n * CH, CH), CH)
        stage[n] = gbuf[n, o, z] + rsr[0, 3, n, o].astype(F32) + rsr[1, 3, n, o].astype(F32)
        last.append(send(stage.at[n], g_out.at[:, cols], d_co))
        g_out[:, cols] = gbuf[n, c, z] + rsr[0, 3, n, c].astype(F32) + rsr[1, 3, n, c].astype(F32)

    ring_forward(L, lb, 4)
    key_all = kb[...].reshape(64, 128)
    val_all = lb[...].reshape(64, 128)
    fold = jnp.where(iota((128, 8), 0) % 8 == iota((128, 8), 1), 1.0, 0.0)
    oi, ki = iota((64, 64), 0), iota((64, 64), 1)
    source = ((ki % 8) // 2) * NZ + ki // 8
    out = jnp.zeros((64, 8), F32)
    for r in range(2):
        want = (2 * dp + r).astype(F32)
        v = hdot(jnp.where(key_all == want, val_all, 0.0), fold)
        out = out + hdot(jnp.where(oi == 2 * source + r, 1.0, 0.0), v)
    lr_out[...] = out

    for copy in last:
        copy.wait_recv()
    for copy in sent:
        copy.wait_send()


def body(hidden_act, readout, log_gap, advantage, version, lengths, routes, weight):
    width = readout.shape[1]
    any_spec = pl.BlockSpec(memory_space=pl.ANY)
    vmem = pl.BlockSpec(memory_space=pltpu.VMEM)
    return tuple(pl.pallas_call(
        functools.partial(kernel, 0.15 / math.sqrt(width)),
        out_shape=(
            jax.ShapeDtypeStruct((64, 8), F32),
            jax.ShapeDtypeStruct((ROWS, 2 * DH), F32),
        ),
        in_specs=[any_spec] * 3 + [vmem] * 5,
        out_specs=(vmem, vmem),
        scratch_shapes=[
            pltpu.VMEM((2, NZ, ROWS, DH), BF),
            pltpu.VMEM((FALL, DH), BF),
            pltpu.VMEM((NY * TOK, DH), BF),
            pltpu.VMEM((TOK, 4 * FB), BF),
            pltpu.VMEM((4 * FB, TOK), BF),
            pltpu.VMEM((2, FB, NY * TOK), BF),
            pltpu.VMEM((2, FB // 2, TOK), BF),
            pltpu.VMEM((NY, 4, 8, 128), F32),
            pltpu.VMEM((NZ, 8, 128), F32),
            pltpu.VMEM((8, 8, 128), F32),
            pltpu.VMEM((NY, 8, 128), F32),
            pltpu.VMEM((NZ, 8, 128), F32),
            pltpu.VMEM((NY * TOK, DH), BF),
            pltpu.VMEM((NCH, 2, NZ, ROWS, CH), F32),
            pltpu.VMEM((2, 4, NCH, 2, ROWS, CH), BF),
            pltpu.VMEM((2, 4, NCH, 2, ROWS, CH), BF),
            pltpu.VMEM((NCH, ROWS, CH), F32),
            pltpu.SemaphoreType.DMA((4,)),
            pltpu.SemaphoreType.DMA((NSEM,)),
            pltpu.SemaphoreType.DMA((NSEM,)),
        ],
        compiler_params=pltpu.CompilerParams(
            collective_id=0, has_side_effects=True, vmem_limit_bytes=60 * 1024 * 1024,
        ),
    )(hidden_act, readout, weight, log_gap, advantage.reshape(1, -1), version.reshape(1, -1),
      lengths, routes))


def solution(mesh):
    placed = (
        P("dp", "mp"),
        P("dp", None),
        P("dp", None),
        P("dp"),
        P("dp"),
        P("dp", None),
        P("dp", None),
        P(("mp", "dp"), None),
    )
    return jax.shard_map(
        body,
        mesh=mesh,
        in_specs=placed,
        out_specs=(P("dp", None), P(("mp", "dp"), None)),
        check_vma=False,
    )
```

time: 525 us -> 84.6 us (0.16)
  waiting for transfers between devices: 372 us -> 0 us
  Pallas kernels: 0 us -> 77.6 us
  starting transfers between devices: 39.1 us -> 0 us
  local copies, waits for them, and re-layouts: 39.1 us -> 6.02 us
  matrix products: 27 us -> 0 us
  blocking collectives: 17.4 us -> 0 us
  between operations: 14.2 us -> 0.64 us
  other arithmetic: 12.3 us -> 0 us
    reduce_scatter x1 -> x0, waiting for transfers between devices: 239 us -> none  [weight_terms(): return lax.psum_scatter(full_term, 'dp', scatter_dimension=0, tiled=True)]
    all_to_all x6 -> x0, waiting for transfers between devices: 132 us -> none  [the longest x1 54.5 us: body(): lax.all_to_all(send_read, 'dp', split_axis=0, concat_axis=0, tiled=True)]
    pallas_call x0 -> x1, Pallas kernels: none -> 77.6 us  [body(): pl.pallas_call(functools.partial(kernel, 0.15 / math.sqrt(width)), out_sh...]
    all_to_all x6 -> x0, starting transfers between devices: 39 us -> none  [the longest x1 12 us: body(): lax.all_to_all(send_stale, 'dp', split_axis=0, concat_axis=0, tiled=True)]
    dot_general x8 -> x0, matrix products: 27 us -> none  [the longest x1 10.6 us: token_shift(): jnp.dot(rows_act, lax.all_gather(weight, 'dp', axis=0, tiled=True), prefe...]
    psum x1 -> x0, blocking collectives: 17.4 us -> none  [token_shift(): return lax.psum(partial_dot, 'mp') * (0.15 / math.sqrt(width))]
    mul x8 -> x0, local copies, waits for them, and re-layouts: 11.8 us -> none  [the longest x3 11.4 us: body(): coef.reshape(-1)[:, None] * scale_out * rows_read.astype(jnp.float32)]
    convert_element_type x2 -> x0, local copies, waits for them, and re-layouts: 9.88 us -> none  [the longest x1 6.57 us: body(): (coef.reshape(-1)[:, None] * scale_out * rows_read.astype(jnp.float32)).a...]
  transfers between devices with their start and end apart: 8 -> 0, of which waited for: 7 -> 0; matrix products, arithmetic and copies ran while one was open for 5% -> 0% of each run, Pallas kernels for 0% -> 0%
where the time goes in v1:
time: 84.6 us; the launch traced here: 84.3 us
  Pallas kernels  77.6 us (92%)
  local copies, waits for them, and re-layouts  6.02 us (7%)
    pallas_call x1, Pallas kernels, body(): pl.pallas_call(functools.partial(kernel, 0.15 / math.sqrt(width)), out_sh...  77.6 us
    unnamed x3, local copies, waits for them, and re-layouts  4.6 us

profile of v1, /device:TPU:1, one launch (start us, length us, event | category | flops | bytes accessed | tf_op | source)
XLA Modules:
  0.0 84.3 jit_solution(17219169002385274111)
XLA Ops:
  0.6 1.4 %copy.10.gap_ref = f32[32,8]{1,0:T(8,128)} copy(f32[32,8]{0,1:T(8,128)} %param.10) | data formatting | bytes 2048 | tf_op args[2]
  2.0 1.3 %copy.11.route_ref = s32[32,1]{1,0:T(8,128)} copy(s32[32,1]{0,1:T(1,128)} %param.14) | data formatting | bytes 256 | tf_op args[6]
  3.3 77.6 %shard_map.95 = (f32[64,8]{1,0:T(8,128)}, f32[56,2560]{1,0:T(8,128)}) custom-call(bf16[256,1792]{1,0:T(8,128)(2,1)} %h_in.1, bf16[256,2560]{1,0:T(8,128)(2,1)} %r_in.1, bf16[56,2560]{1,0:T(8,128)(2,1)} %w_in.1, f32[32,8]{1,0:T(8,128)} %copy.10.gap_ref, f32[1,32]{1,0:T(1,128)} %bitcast.2, s32[1,32]{1,0:T(1,128)} %bitcast.3, s32[1,32]{1,0:T(1,128)} %len_ref.1, ...), custom_call_target="tpu_custom_call" | custom-call | tf_op jit(solution)/shard_map/pallas_call | solution.py:385
  81.0 1.4 %copy.12 = f32[64,8]{0,1:T(8,128)} copy(f32[64,8]{1,0:T(8,128)} %get-tuple-element.2) | data formatting | bytes 4096 | tf_op jit(solution)/shard_map/pallas_call | solution.py:385
  82.4 1.9 %copy.14 = f32[56,2560]{1,0:T(8,128)} copy(f32[56,2560]{1,0:T(8,128)} %get-tuple-element.7) | data formatting | bytes 1146880

commit v2 on v1

--- a/solution.py
+++ b/solution.py
@@ -20,7 +20,7 @@
 FALL = 2 * FB
 CH = 256
 NCH = DH // CH
-NSEM = 140
+NSEM = 190
 
 
 def hdot(a, b):
@@ -34,10 +34,11 @@
     return lax.broadcasted_iota(jnp.int32, shape, dim)
 
 
-def kernel(scale_out, h_in, r_in, w_in, gap_ref, adv_ref, ver_ref, len_ref, route_ref,
+def kernel(scale_out, h_in, r_in, w_in, gap_in, adv_in, ver_in, len_in, route_in,
            lr_out, g_out,
-           wbuf, wcat, rbuf, hv, htr, ht, relay, pkf, kb, ar1, ar2, lb, og, gbuf,
-           rss, rsr, stage, local_sem, send_sem, recv_sem):
+           gap_ref, adv_ref, ver_ref, len_ref, route_ref, lr_buf,
+           wbuf, wfar, wcat, ubuf, rbuf, hv, htr, ht, relay, pkf, kb, ar1, ar2, lb, og, gbuf,
+           rss, rsr, pown, stage, local_sem, send_sem, recv_sem):
     dp = lax.axis_index("dp")
     mp = lax.axis_index("mp")
     y, z = dp // NZ, dp % NZ
@@ -55,6 +56,7 @@
     d_zp, d_zm = dev(y, zp, x, c), dev(y, zm, x, c)
     d_xp, d_xm = dev(y, z, xp, c), dev(y, z, xm, c)
     d_co = dev(y, z, x, o)
+    d_zp_o, d_zm_o = dev(y, zp, x, o), dev(y, zm, x, o)
 
     count = [0]
     sent = []
@@ -80,18 +82,36 @@
     cp_w = pltpu.make_async_copy(w_in.at[:, half], wbuf.at[c, z], local_sem.at[2])
     cp_w.start()
 
+    small = []
+    for i, (a, b) in enumerate((
+            (gap_in, gap_ref), (adv_in, adv_ref), (ver_in, ver_ref), (len_in, len_ref),
+            (route_in, route_ref))):
+        small.append(pltpu.make_async_copy(a, b, local_sem.at[4 + i]))
+        small[-1].start()
+
+    far = (z + 4) % NZ
+    for core in range(2):
+        wbuf[core, far] = jnp.zeros((ROWS, DH), BF)
+
     barrier = pltpu.get_barrier_semaphore()
-    greet = [d_zp, d_zm, d_yp, d_ym, d_y2]
-    greet += [(dp, (mp + k) % 8) for k in range(1, 8)]
+    chips = [(dp, (mp + k) % 8) for k in range(1, 8)]
+    greet = [d_zp, d_zm, d_zp_o, d_zm_o, d_yp, d_ym, d_y2] + chips
     for where in greet:
         pl.semaphore_signal(barrier, inc=1, device_id=where, device_id_type=MESH)
     pl.semaphore_wait(barrier, len(greet))
 
     W = {}
-    w_own = w_in.at[:, half]
-    w_co = send(w_in.at[:, other], wbuf.at[c, z], d_co)
-    W[0, 0, 1] = send(w_own, wbuf.at[c, z], d_zp)
-    W[0, 1, 1] = send(w_own, wbuf.at[c, z], d_zm)
+    WH = DH // 2
+    order = ((0, 0), (1, 1), (0, 1), (1, 0))
+
+    def w_first(k, d, h, where):
+        first = (c if k == 0 else o) * DH + h * WH
+        return send(
+            w_in.at[:, pl.ds(pl.multiple_of(first, 128), WH)],
+            wbuf.at[c, z, :, h * WH:(h + 1) * WH], where)
+
+    for d, h in order:
+        W[0, h, d, 1] = w_first(0, d, h, (d_zp, d_zm)[d])
 
     hb = px * 128
 
@@ -106,8 +126,9 @@
 
     rp_a = r_first(0, d_yp)
     rm_b = r_first(1, d_ym)
-    rp_b = r_first(1, d_yp)
-    rm_a = r_first(0, d_ym)
+    for d, h in order:
+        W[1, h, d, 1] = w_first(1, d, h, (d_zp_o, d_zm_o)[d])
+    w_co = send(w_in.at[:, other], wbuf.at[c, z], d_co)
 
     cp_h.wait()
     for j in range(7):
@@ -122,18 +143,20 @@
     h2p = send(htr.at[h_rows(y2, 0, FB // 2), :], relay.at[0], d_yp)
     h2m = send(htr.at[h_rows(y2, FB // 2, FB // 2), :], relay.at[1], d_ym)
 
-    w_co.wait_recv()
-    W[1, 0, 1] = send(wbuf.at[o, z], wbuf.at[o, z], d_zp)
-    W[1, 1, 1] = send(wbuf.at[o, z], wbuf.at[o, z], d_zm)
+    rp_b = r_first(1, d_yp)
+    rm_a = r_first(0, d_ym)
 
     cp_ho = pltpu.make_async_copy(
         htr.at[h_rows(y, 0, FB), :], ht.at[c, :, cols_at(y)], local_sem.at[3])
     cp_ho.start()
 
-    dest_b = jnp.broadcast_to(route_ref[...].astype(F32), (32, 32))
+    for copy in small:
+        copy.wait()
+    dest_row = route_ref[...].astype(F32)
     ri, ci = iota((32, 32), 0), iota((32, 32), 1)
-    dest_row = jnp.sum(jnp.where(ri == ci, dest_b, 0.0), axis=0, keepdims=True)
-    earlier = jnp.where((dest_b == dest_row) & (ri < ci), 1.0, 0.0)
+    dest_col = jnp.sum(
+        jnp.where(ri == ci, jnp.broadcast_to(dest_row, (32, 32)), 0.0), axis=1, keepdims=True)
+    earlier = jnp.where((dest_col == dest_row) & (ri < ci), 1.0, 0.0)
     rank_row = jnp.sum(earlier, axis=0, keepdims=True)
     key_row = dest_row * 2.0 + rank_row
     ver = ver_ref[...]
@@ -148,7 +171,9 @@
         return hdot(jnp.where(mine8, jnp.broadcast_to(v, (8, 32)), 0.0), spread)
 
     tile = jnp.where(iota((8, 128), 0) == iota((8, 128), 1) % 8, 1.0, 0.0)
-    gap_wide = hdot(gap_ref[...], tile) * spread
+    gap_wide = lax.dot_general(
+        gap_ref[...], tile, (((0,), (0,)), ((), ())), precision=lax.Precision.HIGHEST,
+        preferred_element_type=F32) * spread
     own_rows = iota((8, 128), 0) // 2 == y
     position = (iota((8, 128), 1) % 8).astype(F32)
     len_t = lay(len_ref[...].astype(F32))
@@ -160,14 +185,15 @@
 
     def w_forward(k, s):
         core = c if k == 0 else o
-        for d, where in ((0, d_zp), (1, d_zm)):
-            W[k, d, s].wait_recv()
+        for d, h in order:
+            W[k, h, d, s].wait_recv()
+            if s == 3 and h != d:
+                continue
             origin = (z + (8 - s if d == 0 else s)) % NZ
-            if s < 3:
-                ref = wbuf.at[core, origin]
-            else:
-                ref = wbuf.at[core, origin, :, d * (DH // 2):(d + 1) * (DH // 2)]
-            W[k, d, s + 1] = send(ref, ref, where)
+            cols = slice(h * WH, (h + 1) * WH)
+            src = wbuf.at[core, origin, :, cols]
+            dst = src if s < 3 else wfar.at[core, :, cols]
+            W[k, h, d, s + 1] = send(src, dst, (d_zp, d_zm)[d])
 
     w_forward(0, 1)
 
@@ -182,17 +208,21 @@
     r2b = along(rows_at(yp, 1), d_ym)
     xb = [along(rows_at(yp, 1), d_xp)]
 
-    h1p = send(htr.at[h_rows(yp, 0, FB), :], ht.at[c, :, cols_at(y)], d_yp)
-    h1m = send(htr.at[h_rows(ym, 0, FB), :], ht.at[c, :, cols_at(y)], d_ym)
     cp_ho.wait()
     hp = [send(ht.at[c, :, cols_at(y)], ht.at[c, :, cols_at(y)], d_co)]
 
     w_forward(1, 1)
 
-    rp_b.wait_recv()
-    xb.append(along(rows_at(ym, 1), d_xp))
-    rm_a.wait_recv()
-    xa.append(along(rows_at(yp, 0), d_xm))
+    h2p.wait_recv()
+    hq_p = send(relay.at[0], ht.at[c, 0:FB // 2, cols_at(ym)], d_yp)
+    h2m.wait_recv()
+    hq_m = send(relay.at[1], ht.at[c, FB // 2:FB, cols_at(yp)], d_ym)
+    h1 = []
+    for first in (0, FB // 2):
+        rows = slice(first, first + FB // 2)
+        for to, where in ((yp, d_yp), (ym, d_ym)):
+            h1.append(send(
+                htr.at[h_rows(to, first, FB // 2), :], ht.at[c, rows, cols_at(y)], where))
 
     for copy in pk:
         copy.wait_recv()
@@ -214,44 +244,31 @@
 
     w_forward(0, 2)
 
-    h2p.wait_recv()
-    hq_p = send(relay.at[0], ht.at[c, 0:FB // 2, cols_at(ym)], d_yp)
-    h2m.wait_recv()
-    hq_m = send(relay.at[1], ht.at[c, FB // 2:FB, cols_at(yp)], d_ym)
+    rp_b.wait_recv()
+    xb.append(along(rows_at(ym, 1), d_xp))
+    rm_a.wait_recv()
+    xa.append(along(rows_at(yp, 0), d_xm))
+    ring_forward(K, kb, 1)
 
     w_forward(1, 2)
-    ring_forward(K, kb, 1)
 
     r2a.wait_recv()
     xa.append(along(rows_at(y2, 0), d_xm))
     r2b.wait_recv()
     xb.append(along(rows_at(y2, 1), d_xp))
 
+    ring_forward(K, kb, 2)
     w_forward(0, 3)
-
-    h1p.wait_recv()
-    hp.append(send(ht.at[c, :, cols_at(ym)], ht.at[c, :, cols_at(ym)], d_co))
-    h1m.wait_recv()
-    hp.append(send(ht.at[c, :, cols_at(yp)], ht.at[c, :, cols_at(yp)], d_co))
-
-    w_forward(1, 3)
-    ring_forward(K, kb, 2)
 
     hq_p.wait_recv()
     hq_m.wait_recv()
     hp.append(send(ht.at[c, :, cols_at(y2)], ht.at[c, :, cols_at(y2)], d_co))
 
-    cp_r.wait()
+    w_forward(1, 3)
+    ring_forward(K, kb, 3)
+
     cp_w.wait()
-    for copy in xa + xb:
-        copy.wait_recv()
-    for k in range(2):
-        for d in range(2):
-            W[k, d, 4].wait_recv()
-    ring_forward(K, kb, 3)
-    for copy in hp:
-        copy.wait_recv()
-
+    w_co.wait_recv()
     for core in range(2):
         for j in range(NZ // 2):
             for n in range(NCH):
@@ -261,19 +278,28 @@
                      wbuf[core, 2 * j + 1, :, cols].astype(F32)], axis=0)
                 first = core * FB + 2 * j * ROWS
                 wcat[first:first + 2 * ROWS, cols] = pair.astype(BF)
-    parts = []
-    for b in range(NY):
-        u = lax.dot_general(
-            wcat[...], rbuf[b * TOK:(b + 1) * TOK, :], (((1,), (1,)), ((), ())),
-            preferred_element_type=F32,
-        )
-        h = ht[:, :, b * TOK:(b + 1) * TOK].reshape(FALL, TOK).astype(F32)
-        s = jnp.sum(u * h, axis=0, keepdims=True)
-        parts += [s[:, 0:128], s[:, 128:256]]
-    ar1[mp] = jnp.concatenate(parts, axis=0)
-    first_stage = [
-        send(ar1.at[mp], ar1.at[mp], (dp, (mp + k) % 8)) for k in range(1, 8)
-    ]
+
+    def contract(w, r):
+        return lax.dot_general(w, r, (((1,), (1,)), ((), ())), preferred_element_type=F32)
+
+    def block(yy):
+        ubuf[yy] = contract(wcat[...], rbuf[pl.ds(pl.multiple_of(yy * TOK, TOK), TOK), :])
+
+    cp_r.wait()
+    block(y)
+    for copy in (xa[0], xb[0], xa[1], xb[1]):
+        copy.wait_recv()
+    block(ym)
+    block(yp)
+    for i in range(2):
+        rows = slice(i * (FB // 2), (i + 1) * (FB // 2))
+        for j, yy in ((0, ym), (1, yp)):
+            h1[2 * i + j].wait_recv()
+            ref = ht.at[c, rows, cols_at(yy)]
+            hp.append(send(ref, ref, d_co))
+    xa[2].wait_recv()
+    xb[2].wait_recv()
+    block(y2)
     ring_forward(K, kb, 4)
 
     keys = [jnp.floor(kb[i] * 0.5) for i in range(NZ)]
@@ -286,14 +312,34 @@
         total = jnp.sum(jnp.sum(hits, axis=0, keepdims=True), axis=1, keepdims=True)
         count_each = jnp.where(own_dest == float(k), jnp.broadcast_to(total, (8, 128)), count_each)
 
-    for copy in first_stage:
+    for k in range(2):
+        for d in range(2):
+            W[k, d, d, 4].wait_recv()
+    shifted = far % 2 == 1
+    first = pl.multiple_of(far * ROWS - 8 * (far % 2), 16)
+    for copy in hp:
         copy.wait_recv()
-    acc = ar1[0]
-    for i in range(1, 8):
-        acc = acc + ar1[i]
-    ar2[y] = acc
-    second_stage = [send(ar2.at[y], ar2.at[y], d) for d in (d_yp, d_ym, d_y2)]
-    for copy in second_stage:
+    total = jnp.zeros((1, NY * TOK), F32)
+    pad = jnp.zeros((8, DH), F32)
+    for core in range(2):
+        w = wfar[core].astype(F32)
+        w = jnp.where(shifted, jnp.concatenate([pad, w], 0), jnp.concatenate([w, pad], 0))
+        u = contract(w.astype(BF), rbuf[...])
+        total = total + jnp.sum(
+            u * ht[core, pl.ds(first, 64), :].astype(F32), axis=0, keepdims=True)
+    parts = []
+    for b in range(NY):
+        h = ht[:, :, b * TOK:(b + 1) * TOK].reshape(FALL, TOK).astype(F32)
+        s = total[:, b * TOK:(b + 1) * TOK] + jnp.sum(ubuf[b] * h, axis=0, keepdims=True)
+        parts += [s[:, 0:128], s[:, 128:256]]
+    ar1[mp] = jnp.concatenate(parts, axis=0)
+    partial = [send(ar1.at[mp], ar1.at[mp], where) for where in chips]
+
+    for copy in partial:
+        copy.wait_recv()
+    ar2[y] = ((ar1[0] + ar1[1]) + (ar1[2] + ar1[3])) + ((ar1[4] + ar1[5]) + (ar1[6] + ar1[7]))
+    partial = [send(ar2.at[y], ar2.at[y], where) for where in (d_yp, d_ym, d_y2)]
+    for copy in partial:
         copy.wait_recv()
     total = (ar2[0] + ar2[1]) + (ar2[2] + ar2[3])
 
@@ -316,7 +362,6 @@
 
     ends = ((0, d_zp), (1, d_zm))
     sides = (slice(0, CH // 2), slice(CH // 2, CH))
-    far = (z + 4) % NZ
     hall = ht[...].reshape(FALL, NY * TOK)
     for n in range(NCH):
         cols = slice(n * CH, (n + 1) * CH)
@@ -328,6 +373,7 @@
         for d, where in ends:
             rss[d, 0, n, :, :, sides[d]] = gbuf[n, :, far, :, sides[d]].astype(BF)
             push(d, 1, n, sides[d], where)
+    shares = [send(gbuf.at[n, o, z], pown.at[n], d_co) for n in range(NCH)]
 
     L = {}
     L[0, 1] = send(lb.at[z], lb.at[z], d_zp)
@@ -347,17 +393,14 @@
                 else:
                     rss[d, s - 1, n] = (
                         gbuf[n, :, to] + rsr[d, s - 2, n].astype(F32)).astype(BF)
-                push(d, s, n, full, where)
+                if s < 4:
+                    push(d, s, n, full, where)
+                else:
+                    RS[d, 4, n] = [
+                        send(rss.at[d, 3, n, c], rsr.at[d, 3, n, 0], where),
+                        send(rss.at[d, 3, n, o], rsr.at[d, 3, n, 1], (d_zp_o, d_zm_o)[d]),
+                    ]
         ring_forward(L, lb, s - 1)
-
-    last = []
-    for n in range(NCH):
-        for d, _ in ends:
-            RS[d, 4, n].wait_recv()
-        cols = pl.ds(pl.multiple_of(c * DH + n * CH, CH), CH)
-        stage[n] = gbuf[n, o, z] + rsr[0, 3, n, o].astype(F32) + rsr[1, 3, n, o].astype(F32)
-        last.append(send(stage.at[n], g_out.at[:, cols], d_co))
-        g_out[:, cols] = gbuf[n, c, z] + rsr[0, 3, n, c].astype(F32) + rsr[1, 3, n, c].astype(F32)
 
     ring_forward(L, lb, 4)
     key_all = kb[...].reshape(64, 128)
@@ -370,29 +413,54 @@
         want = (2 * dp + r).astype(F32)
         v = hdot(jnp.where(key_all == want, val_all, 0.0), fold)
         out = out + hdot(jnp.where(oi == 2 * source + r, 1.0, 0.0), v)
-    lr_out[...] = out
-
-    for copy in last:
-        copy.wait_recv()
+    lr_buf[...] = out.T
+    outs = [pltpu.make_async_copy(lr_buf, lr_out, local_sem.at[9])]
+    outs[0].start()
+
+    for n in range(NCH):
+        shares[n].wait_recv()
+        for d, _ in ends:
+            for copy in RS[d, 4, n]:
+                copy.wait_recv()
+        stage[0, n] = gbuf[n, c, z] + rsr[0, 3, n, 0].astype(F32) + rsr[1, 3, n, 0].astype(F32)
+        stage[1, n] = pown[n] + rsr[0, 3, n, 1].astype(F32) + rsr[1, 3, n, 1].astype(F32)
+        for i, core in enumerate((c, o)):
+            cols = pl.ds(pl.multiple_of(core * DH + n * CH, CH), CH)
+            out = pltpu.make_async_copy(
+                stage.at[i, n], g_out.at[:, cols], local_sem.at[10 + 2 * n + i])
+            out.start()
+            outs.append(out)
+
+    for copy in outs:
+        copy.wait()
     for copy in sent:
         copy.wait_send()
+    assert count[0] <= NSEM, count[0]
 
 
 def body(hidden_act, readout, log_gap, advantage, version, lengths, routes, weight):
     width = readout.shape[1]
     any_spec = pl.BlockSpec(memory_space=pl.ANY)
     vmem = pl.BlockSpec(memory_space=pltpu.VMEM)
-    return tuple(pl.pallas_call(
+    lr, grad = pl.pallas_call(
         functools.partial(kernel, 0.15 / math.sqrt(width)),
         out_shape=(
-            jax.ShapeDtypeStruct((64, 8), F32),
+            jax.ShapeDtypeStruct((8, 64), F32),
             jax.ShapeDtypeStruct((ROWS, 2 * DH), F32),
         ),
-        in_specs=[any_spec] * 3 + [vmem] * 5,
-        out_specs=(vmem, vmem),
+        in_specs=[any_spec] * 8,
+        out_specs=(any_spec, any_spec),
         scratch_shapes=[
+            pltpu.VMEM((8, 32), F32),
+            pltpu.VMEM((1, 32), F32),
+            pltpu.VMEM((1, 32), jnp.int32),
+            pltpu.VMEM((1, 32), jnp.int32),
+            pltpu.VMEM((1, 32), jnp.int32),
+            pltpu.VMEM((8, 64), F32),
             pltpu.VMEM((2, NZ, ROWS, DH), BF),
+            pltpu.VMEM((2, ROWS, DH), BF),
             pltpu.VMEM((FALL, DH), BF),
+            pltpu.VMEM((NY, FALL, TOK), F32),
             pltpu.VMEM((NY * TOK, DH), BF),
             pltpu.VMEM((TOK, 4 * FB), BF),
             pltpu.VMEM((4 * FB, TOK), BF),
@@ -408,15 +476,31 @@
             pltpu.VMEM((2, 4, NCH, 2, ROWS, CH), BF),
             pltpu.VMEM((2, 4, NCH, 2, ROWS, CH), BF),
             pltpu.VMEM((NCH, ROWS, CH), F32),
-            pltpu.SemaphoreType.DMA((4,)),
+            pltpu.VMEM((2, NCH, ROWS, CH), F32),
+            pltpu.SemaphoreType.DMA((20,)),
             pltpu.SemaphoreType.DMA((NSEM,)),
             pltpu.SemaphoreType.DMA((NSEM,)),
         ],
         compiler_params=pltpu.CompilerParams(
             collective_id=0, has_side_effects=True, vmem_limit_bytes=60 * 1024 * 1024,
         ),
-    )(hidden_act, readout, weight, log_gap, advantage.reshape(1, -1), version.reshape(1, -1),
-      lengths, routes))
+    )(hidden_act, readout, weight, log_gap.T, advantage.reshape(1, -1), version.reshape(1, -1),
+      lengths, routes.reshape(1, -1))
+    lr, grad = pl.pallas_call(
+        hand_over,
+        out_shape=(
+            jax.ShapeDtypeStruct((8, 64), F32),
+            jax.ShapeDtypeStruct((ROWS, 2 * DH), F32),
+        ),
+        in_specs=[vmem, vmem],
+        out_specs=(vmem, vmem),
+    )(lr, grad)
+    return lr.T, grad
+
+
+def hand_over(lr_in, g_in, lr_out, g_out):
+    lr_out[...] = lr_in[...]
+    g_out[...] = g_in[...]
 
 
 def solution(mesh):

time: 84.6 us -> 80.3 us (0.949)
  local copies, waits for them, and re-layouts: 6.02 us -> 0 us
  Pallas kernels: 77.6 us -> 79.5 us
    unnamed x3 -> x0, local copies, waits for them, and re-layouts: 4.6 us -> none
    pallas_call x0 -> x1, Pallas kernels: none -> 1.91 us  [body(): pl.pallas_call(hand_over, out_shape=(jax.ShapeDtypeStruct((8, 64), F32),...]
    pallas_call x1 -> x0, local copies, waits for them, and re-layouts: 1.42 us -> none  [body(): pl.pallas_call(functools.partial(kernel, 0.15 / math.sqrt(width)), out_sh...]
where the time goes in v2:
time: 80.3 us; the launch traced here: 80.1 us
  Pallas kernels  79.5 us (99%)
    pallas_call x1, Pallas kernels, body(): pl.pallas_call(functools.partial(kernel, 0.15 / math.sqrt(width)), out_sh...  77.6 us
    pallas_call x1, Pallas kernels, body(): pl.pallas_call(hand_over, out_shape=(jax.ShapeDtypeStruct((8, 64), F32),...  1.91 us

profile of v2, /device:TPU:1, one launch (start us, length us, event | category | flops | bytes accessed | tf_op | source)
XLA Modules:
  0.0 80.1 jit_solution(13166240788632840703)
XLA Ops:
  0.6 77.6 %shard_map.95 = (f32[8,64]{1,0:T(8,128)}, f32[56,2560]{1,0:T(8,128)}) custom-call(bf16[256,1792]{1,0:T(8,128)(2,1)} %h_in.1, bf16[256,2560]{1,0:T(8,128)(2,1)} %r_in.1, bf16[56,2560]{1,0:T(8,128)(2,1)} %w_in.1, f32[8,32]{1,0:T(8,128)} %bitcast.5, f32[1,32]{1,0:T(1,128)} %bitcast.6, s32[1,32]{1,0:T(1,128)} %bitcast.7, s32[1,32]{1,0:T(1,128)} %len_in.1, ...), custom_call_target="tpu_custom_call" | custom-call | tf_op jit(solution)/shard_map/pallas_call | solution.py:445
  78.2 1.9 %shard_map.96 = (f32[8,64]{1,0:T(8,128)}, f32[56,2560]{1,0:T(8,128)}) custom-call(f32[8,64]{1,0:T(8,128)} %get-tuple-element.6.lr_in, f32[56,2560]{1,0:T(8,128)} %get-tuple-element.7.g_in), custom_call_target="tpu_custom_call" | custom-call | tf_op jit(solution)/shard_map/pallas_call | solution.py:489

commit v3 on v2

--- a/solution.py
+++ b/solution.py
@@ -16,11 +16,13 @@
 TOK = 256
 DH = 1280
 ROWS = 56
+PAIR = 2 * ROWS
 FB = ROWS * NZ
 FALL = 2 * FB
+CHUNKS = tuple((i * 256, 256) for i in range(5))
 CH = 256
-NCH = DH // CH
-NSEM = 190
+NCH = len(CHUNKS)
+NSEM = 200
 
 
 def hdot(a, b):
@@ -37,7 +39,7 @@
 def kernel(scale_out, h_in, r_in, w_in, gap_in, adv_in, ver_in, len_in, route_in,
            lr_out, g_out,
            gap_ref, adv_ref, ver_ref, len_ref, route_ref, lr_buf,
-           wbuf, wfar, wcat, ubuf, rbuf, hv, htr, ht, relay, pkf, kb, ar1, ar2, lb, og, gbuf,
+           wbuf, wcat, ubuf, acc, rbuf, hv, htr, ht, relay, pkf, kb, ar1, ar2, lb, og, gbuf,
            rss, rsr, pown, stage, local_sem, send_sem, recv_sem):
     dp = lax.axis_index("dp")
     mp = lax.axis_index("mp")
@@ -90,8 +92,6 @@
         small[-1].start()
 
     far = (z + 4) % NZ
-    for core in range(2):
-        wbuf[core, far] = jnp.zeros((ROWS, DH), BF)
 
     barrier = pltpu.get_barrier_semaphore()
     chips = [(dp, (mp + k) % 8) for k in range(1, 8)]
@@ -126,6 +126,8 @@
 
     rp_a = r_first(0, d_yp)
     rm_b = r_first(1, d_ym)
+    rp_b = r_first(1, d_yp)
+    rm_a = r_first(0, d_ym)
     for d, h in order:
         W[1, h, d, 1] = w_first(1, d, h, (d_zp_o, d_zm_o)[d])
     w_co = send(w_in.at[:, other], wbuf.at[c, z], d_co)
@@ -139,12 +141,6 @@
 
     def cols_at(yy):
         return pl.ds(pl.multiple_of(yy * TOK, TOK), TOK)
-
-    h2p = send(htr.at[h_rows(y2, 0, FB // 2), :], relay.at[0], d_yp)
-    h2m = send(htr.at[h_rows(y2, FB // 2, FB // 2), :], relay.at[1], d_ym)
-
-    rp_b = r_first(1, d_yp)
-    rm_a = r_first(0, d_ym)
 
     cp_ho = pltpu.make_async_copy(
         htr.at[h_rows(y, 0, FB), :], ht.at[c, :, cols_at(y)], local_sem.at[3])
@@ -181,6 +177,12 @@
     pkf[y, 1] = jnp.where(own_rows & (position >= len_t), -1.0, lay(key_row))
     pkf[y, 2] = lay(adv_ref[...])
     pkf[y, 3] = lay(stale_row)
+    len_col = jnp.sum(
+        jnp.where(ri == ci, jnp.broadcast_to(len_ref[...].astype(F32), (32, 32)), 0.0),
+        axis=1, keepdims=True)
+    shard_hit = dest_col == iota((32, 128), 1).astype(F32)
+    here = jnp.sum(jnp.where(shard_hit, len_col, 0.0), axis=0, keepdims=True)
+    pkf[y, 4] = jnp.broadcast_to(here, (8, 128))
     pk = [send(pkf.at[y], pkf.at[y], d) for d in (d_yp, d_ym, d_y2)]
 
     def w_forward(k, s):
@@ -192,42 +194,57 @@
             origin = (z + (8 - s if d == 0 else s)) % NZ
             cols = slice(h * WH, (h + 1) * WH)
             src = wbuf.at[core, origin, :, cols]
-            dst = src if s < 3 else wfar.at[core, :, cols]
-            W[k, h, d, s + 1] = send(src, dst, (d_zp, d_zm)[d])
+            W[k, h, d, s + 1] = send(src, src, (d_zp, d_zm)[d])
 
     w_forward(0, 1)
+
+    pairs = [(z // 2 + step) % 4 for step in (0, 1, 3, 2)]
+
+    def build(p, core):
+        for n in range(5):
+            cols = slice(n * 256, (n + 1) * 256)
+            pair = jnp.concatenate(
+                [wbuf[core, 2 * pairs[p], :, cols].astype(F32),
+                 wbuf[core, 2 * pairs[p] + 1, :, cols].astype(F32)], axis=0)
+            wcat[p, core, :, cols] = pair.astype(BF)
 
     def along(ref_rows, where):
         ref = rbuf.at[ref_rows, :]
         return send(ref, ref, where)
 
+    def piece(yy, part, i):
+        first = yy * TOK + hb + part * 64 + i * 32
+        return pl.ds(pl.multiple_of(first, 32), 32)
+
     rp_a.wait_recv()
-    r2a = along(rows_at(ym, 0), d_yp)
+    r2a = [along(piece(ym, 0, i), d_yp) for i in range(2)]
     xa = [along(rows_at(ym, 0), d_xm)]
     rm_b.wait_recv()
-    r2b = along(rows_at(yp, 1), d_ym)
+    r2b = [along(piece(yp, 1, i), d_ym) for i in range(2)]
     xb = [along(rows_at(yp, 1), d_xp)]
-
-    cp_ho.wait()
-    hp = [send(ht.at[c, :, cols_at(y)], ht.at[c, :, cols_at(y)], d_co)]
-
-    w_forward(1, 1)
-
-    h2p.wait_recv()
-    hq_p = send(relay.at[0], ht.at[c, 0:FB // 2, cols_at(ym)], d_yp)
-    h2m.wait_recv()
-    hq_m = send(relay.at[1], ht.at[c, FB // 2:FB, cols_at(yp)], d_ym)
+    h2p = send(htr.at[h_rows(y2, 0, FB // 2), :], relay.at[0], d_yp)
+    h2m = send(htr.at[h_rows(y2, FB // 2, FB // 2), :], relay.at[1], d_ym)
     h1 = []
     for first in (0, FB // 2):
         rows = slice(first, first + FB // 2)
         for to, where in ((yp, d_yp), (ym, d_ym)):
             h1.append(send(
                 htr.at[h_rows(to, first, FB // 2), :], ht.at[c, rows, cols_at(y)], where))
+    cp_ho.wait()
+    hp = [send(ht.at[c, :, cols_at(y)], ht.at[c, :, cols_at(y)], d_co)]
+
+    w_forward(1, 1)
+
+    rp_b.wait_recv()
+    xb.append(along(rows_at(ym, 1), d_xp))
+    rm_a.wait_recv()
+    xa.append(along(rows_at(yp, 0), d_xm))
 
     for copy in pk:
         copy.wait_recv()
-    fields = [pkf[0, f] + pkf[1, f] + pkf[2, f] + pkf[3, f] for f in range(4)]
-    kb[z] = fields[1]
+    fields = [pkf[0, f] + pkf[1, f] + pkf[2, f] + pkf[3, f] for f in range(5)]
+    kb[z, 0] = fields[1]
+    kb[z, 1] = fields[4]
     K = {}
     K[0, 1] = send(kb.at[z], kb.at[z], d_zp)
     K[1, 1] = send(kb.at[z], kb.at[z], d_zm)
@@ -242,98 +259,101 @@
             origin = (z + (8 - s if d == 0 else s)) % NZ
             table[d, s + 1] = send(buf.at[origin], buf.at[origin], where)
 
+    cp_w.wait()
+    w_co.wait_recv()
+    build(0, c)
+    build(0, o)
     w_forward(0, 2)
-
-    rp_b.wait_recv()
-    xb.append(along(rows_at(ym, 1), d_xp))
-    rm_a.wait_recv()
-    xa.append(along(rows_at(yp, 0), d_xm))
     ring_forward(K, kb, 1)
 
+    for i in range(2):
+        r2a[i].wait_recv()
+        xa.append(along(piece(y2, 0, i), d_xm))
+        r2b[i].wait_recv()
+        xb.append(along(piece(y2, 1, i), d_xp))
+
     w_forward(1, 2)
-
-    r2a.wait_recv()
-    xa.append(along(rows_at(y2, 0), d_xm))
-    r2b.wait_recv()
-    xb.append(along(rows_at(y2, 1), d_xp))
-
     ring_forward(K, kb, 2)
+
+    h2p.wait_recv()
+    hq_p = send(relay.at[0], ht.at[c, 0:FB // 2, cols_at(ym)], d_yp)
+    h2m.wait_recv()
+    hq_m = send(relay.at[1], ht.at[c, FB // 2:FB, cols_at(yp)], d_ym)
+
     w_forward(0, 3)
-
-    hq_p.wait_recv()
-    hq_m.wait_recv()
-    hp.append(send(ht.at[c, :, cols_at(y2)], ht.at[c, :, cols_at(y2)], d_co))
-
+    build(1, c)
+    build(2, c)
     w_forward(1, 3)
     ring_forward(K, kb, 3)
 
-    cp_w.wait()
-    w_co.wait_recv()
-    for core in range(2):
-        for j in range(NZ // 2):
-            for n in range(NCH):
-                cols = slice(n * CH, (n + 1) * CH)
-                pair = jnp.concatenate(
-                    [wbuf[core, 2 * j, :, cols].astype(F32),
-                     wbuf[core, 2 * j + 1, :, cols].astype(F32)], axis=0)
-                first = core * FB + 2 * j * ROWS
-                wcat[first:first + 2 * ROWS, cols] = pair.astype(BF)
+    build(1, o)
+    build(2, o)
 
     def contract(w, r):
         return lax.dot_general(w, r, (((1,), (1,)), ((), ())), preferred_element_type=F32)
 
     def block(yy):
-        ubuf[yy] = contract(wcat[...], rbuf[pl.ds(pl.multiple_of(yy * TOK, TOK), TOK), :])
-
-    cp_r.wait()
-    block(y)
-    for copy in (xa[0], xb[0], xa[1], xb[1]):
-        copy.wait_recv()
-    block(ym)
-    block(yp)
+        ubuf[yy] = contract(
+            wcat[0:3].reshape(6 * PAIR, DH),
+            rbuf[pl.ds(pl.multiple_of(yy * TOK, TOK), TOK), :])
+
+    def hidden(p, yy):
+        rows = pl.ds(pl.multiple_of(pairs[p] * PAIR, 16), PAIR)
+        return ht[:, rows, cols_at(yy)].reshape(2 * PAIR, TOK).astype(F32)
+
+    def row_dot(yy):
+        total = jnp.zeros((1, TOK), F32)
+        for p in range(3):
+            u = ubuf[yy, p * 2 * PAIR:(p + 1) * 2 * PAIR, :]
+            total = total + jnp.sum(u * hidden(p, yy), axis=0, keepdims=True)
+        acc[yy] = total
+
     for i in range(2):
         rows = slice(i * (FB // 2), (i + 1) * (FB // 2))
         for j, yy in ((0, ym), (1, yp)):
             h1[2 * i + j].wait_recv()
             ref = ht.at[c, rows, cols_at(yy)]
             hp.append(send(ref, ref, d_co))
-    xa[2].wait_recv()
-    xb[2].wait_recv()
+    cp_r.wait()
+    block(y)
+    hq_p.wait_recv()
+    hq_m.wait_recv()
+    hp.append(send(ht.at[c, :, cols_at(y2)], ht.at[c, :, cols_at(y2)], d_co))
+    for copy in (xa[0], xb[0], xa[1], xb[1]):
+        copy.wait_recv()
+    block(ym)
+    block(yp)
+    for copy in xa[2:] + xb[2:]:
+        copy.wait_recv()
     block(y2)
     ring_forward(K, kb, 4)
-
-    keys = [jnp.floor(kb[i] * 0.5) for i in range(NZ)]
+    for copy in hp[:5]:
+        copy.wait_recv()
+    row_dot(y)
+    row_dot(ym)
+    row_dot(yp)
+    hp[5].wait_recv()
+    row_dot(y2)
+
+    for k, core in ((0, c), (1, o)):
+        for d in range(2):
+            W[k, d, d, 4].wait_recv()
+        build(3, core)
+    parts = []
+    for b in range(NY):
+        u = contract(wcat[3].reshape(2 * PAIR, DH), rbuf[b * TOK:(b + 1) * TOK, :])
+        s = acc[b] + jnp.sum(u * hidden(3, b), axis=0, keepdims=True)
+        parts += [s[:, 0:128], s[:, 128:256]]
+    ar1[mp] = jnp.concatenate(parts, axis=0)
+    partial = [send(ar1.at[mp], ar1.at[mp], where) for where in chips]
+
+    tally = kb[0, 1]
+    for i in range(1, NZ):
+        tally = tally + kb[i, 1]
     own_dest = jnp.floor(fields[1] * 0.5)
     count_each = jnp.ones((8, 128), F32)
     for k in range(NY * NZ):
-        hits = jnp.zeros((8, 128), F32)
-        for i in range(NZ):
-            hits = hits + jnp.where(keys[i] == float(k), 1.0, 0.0)
-        total = jnp.sum(jnp.sum(hits, axis=0, keepdims=True), axis=1, keepdims=True)
-        count_each = jnp.where(own_dest == float(k), jnp.broadcast_to(total, (8, 128)), count_each)
-
-    for k in range(2):
-        for d in range(2):
-            W[k, d, d, 4].wait_recv()
-    shifted = far % 2 == 1
-    first = pl.multiple_of(far * ROWS - 8 * (far % 2), 16)
-    for copy in hp:
-        copy.wait_recv()
-    total = jnp.zeros((1, NY * TOK), F32)
-    pad = jnp.zeros((8, DH), F32)
-    for core in range(2):
-        w = wfar[core].astype(F32)
-        w = jnp.where(shifted, jnp.concatenate([pad, w], 0), jnp.concatenate([w, pad], 0))
-        u = contract(w.astype(BF), rbuf[...])
-        total = total + jnp.sum(
-            u * ht[core, pl.ds(first, 64), :].astype(F32), axis=0, keepdims=True)
-    parts = []
-    for b in range(NY):
-        h = ht[:, :, b * TOK:(b + 1) * TOK].reshape(FALL, TOK).astype(F32)
-        s = total[:, b * TOK:(b + 1) * TOK] + jnp.sum(ubuf[b] * h, axis=0, keepdims=True)
-        parts += [s[:, 0:128], s[:, 128:256]]
-    ar1[mp] = jnp.concatenate(parts, axis=0)
-    partial = [send(ar1.at[mp], ar1.at[mp], where) for where in chips]
+        count_each = jnp.where(own_dest == float(k), tally[:, k:k + 1], count_each)
 
     for copy in partial:
         copy.wait_recv()
@@ -343,7 +363,7 @@
         copy.wait_recv()
     total = (ar2[0] + ar2[1]) + (ar2[2] + ar2[3])
 
-    gap, key, adv, stale = fields
+    gap, key, adv, stale = fields[:4]
     live = key >= 0.0
     logit = gap + total * scale_out
     lb[z] = jnp.where(live, logit, 0.0)
@@ -357,53 +377,54 @@
 
     RS = {}
 
-    def push(d, s, n, cols, where):
-        RS[d, s, n] = send(rss.at[d, s - 1, n, :, :, cols], rsr.at[d, s - 1, n, :, :, cols], where)
-
     ends = ((0, d_zp), (1, d_zm))
-    sides = (slice(0, CH // 2), slice(CH // 2, CH))
     hall = ht[...].reshape(FALL, NY * TOK)
-    for n in range(NCH):
-        cols = slice(n * CH, (n + 1) * CH)
+    for n, (start, wide) in enumerate(CHUNKS):
+        cols = slice(start, start + wide)
         for b in range(8):
             rows = slice(b * 128, (b + 1) * 128)
             og[rows, cols] = (coef_col[:, b:b + 1] * rbuf[rows, cols].astype(F32)).astype(BF)
         g = jnp.dot(hall, og[:, cols], preferred_element_type=F32)
-        gbuf[n] = g.reshape(2, NZ, ROWS, CH)
+        w = slice(0, wide)
+        gbuf[n, :, :, :, w] = g.reshape(2, NZ, ROWS, wide)
         for d, where in ends:
-            rss[d, 0, n, :, :, sides[d]] = gbuf[n, :, far, :, sides[d]].astype(BF)
-            push(d, 1, n, sides[d], where)
-    shares = [send(gbuf.at[n, o, z], pown.at[n], d_co) for n in range(NCH)]
+            rss[d, 0, n, d, :, w] = gbuf[n, d, far, :, w].astype(BF)
+            RS[d, 1, n] = send(rss.at[d, 0, n, d, :, w], rsr.at[d, 0, n, d, :, w], where)
+    shares = [
+        send(gbuf.at[n, o, z, :, 0:CHUNKS[n][1]], pown.at[n, :, 0:CHUNKS[n][1]], d_co)
+        for n in range(NCH)
+    ]
 
     L = {}
     L[0, 1] = send(lb.at[z], lb.at[z], d_zp)
     L[1, 1] = send(lb.at[z], lb.at[z], d_zm)
 
-    full = slice(0, CH)
     for s in range(2, 5):
-        for n in range(NCH):
+        for n, (start, wide) in enumerate(CHUNKS):
+            w = slice(0, wide)
             for d, where in ends:
                 to = (z + (5 - s if d == 0 else 3 + s)) % NZ
                 RS[d, s - 1, n].wait_recv()
                 if s == 2:
-                    a, b = sides[d], sides[1 - d]
-                    rss[d, 1, n, :, :, a] = (
-                        gbuf[n, :, to, :, a] + rsr[d, 0, n, :, :, a].astype(F32)).astype(BF)
-                    rss[d, 1, n, :, :, b] = gbuf[n, :, to, :, b].astype(BF)
+                    rss[d, 1, n, d, :, w] = (
+                        gbuf[n, d, to, :, w] + rsr[d, 0, n, d, :, w].astype(F32)).astype(BF)
+                    rss[d, 1, n, 1 - d, :, w] = gbuf[n, 1 - d, to, :, w].astype(BF)
                 else:
-                    rss[d, s - 1, n] = (
-                        gbuf[n, :, to] + rsr[d, s - 2, n].astype(F32)).astype(BF)
+                    rss[d, s - 1, n, :, :, w] = (
+                        gbuf[n, :, to, :, w] + rsr[d, s - 2, n, :, :, w].astype(F32)).astype(BF)
                 if s < 4:
-                    push(d, s, n, full, where)
+                    RS[d, s, n] = send(
+                        rss.at[d, s - 1, n, :, :, w], rsr.at[d, s - 1, n, :, :, w], where)
                 else:
                     RS[d, 4, n] = [
-                        send(rss.at[d, 3, n, c], rsr.at[d, 3, n, 0], where),
-                        send(rss.at[d, 3, n, o], rsr.at[d, 3, n, 1], (d_zp_o, d_zm_o)[d]),
+                        send(rss.at[d, 3, n, c, :, w], rsr.at[d, 3, n, 0, :, w], where),
+                        send(rss.at[d, 3, n, o, :, w], rsr.at[d, 3, n, 1, :, w],
+                             (d_zp_o, d_zm_o)[d]),
                     ]
         ring_forward(L, lb, s - 1)
 
     ring_forward(L, lb, 4)
-    key_all = kb[...].reshape(64, 128)
+    key_all = kb[:, 0].reshape(64, 128)
     val_all = lb[...].reshape(64, 128)
     fold = jnp.where(iota((128, 8), 0) % 8 == iota((128, 8), 1), 1.0, 0.0)
     oi, ki = iota((64, 64), 0), iota((64, 64), 1)
@@ -417,17 +438,18 @@
     outs = [pltpu.make_async_copy(lr_buf, lr_out, local_sem.at[9])]
     outs[0].start()
 
-    for n in range(NCH):
+    for n, (start, wide) in enumerate(CHUNKS):
+        w = slice(0, wide)
         shares[n].wait_recv()
         for d, _ in ends:
             for copy in RS[d, 4, n]:
                 copy.wait_recv()
-        stage[0, n] = gbuf[n, c, z] + rsr[0, 3, n, 0].astype(F32) + rsr[1, 3, n, 0].astype(F32)
-        stage[1, n] = pown[n] + rsr[0, 3, n, 1].astype(F32) + rsr[1, 3, n, 1].astype(F32)
-        for i, core in enumerate((c, o)):
-            cols = pl.ds(pl.multiple_of(core * DH + n * CH, CH), CH)
+        for i, (core, own) in enumerate(((c, gbuf[n, c, z, :, w]), (o, pown[n, :, w]))):
+            stage[i, n, :, w] = (
+                own + rsr[0, 3, n, i, :, w].astype(F32) + rsr[1, 3, n, i, :, w].astype(F32))
+            cols = pl.ds(pl.multiple_of(core * DH + start, 128), wide)
             out = pltpu.make_async_copy(
-                stage.at[i, n], g_out.at[:, cols], local_sem.at[10 + 2 * n + i])
+                stage.at[i, n, :, w], g_out.at[:, cols], local_sem.at[10 + 2 * n + i])
             out.start()
             outs.append(out)
 
@@ -458,16 +480,16 @@
             pltpu.VMEM((1, 32), jnp.int32),
             pltpu.VMEM((8, 64), F32),
             pltpu.VMEM((2, NZ, ROWS, DH), BF),
-            pltpu.VMEM((2, ROWS, DH), BF),
-            pltpu.VMEM((FALL, DH), BF),
-            pltpu.VMEM((NY, FALL, TOK), F32),
+            pltpu.VMEM((4, 2, PAIR, DH), BF),
+            pltpu.VMEM((NY, 6 * PAIR, TOK), F32),
+            pltpu.VMEM((NY, 1, TOK), F32),
             pltpu.VMEM((NY * TOK, DH), BF),
             pltpu.VMEM((TOK, 4 * FB), BF),
             pltpu.VMEM((4 * FB, TOK), BF),
             pltpu.VMEM((2, FB, NY * TOK), BF),
             pltpu.VMEM((2, FB // 2, TOK), BF),
-            pltpu.VMEM((NY, 4, 8, 128), F32),
-            pltpu.VMEM((NZ, 8, 128), F32),
+            pltpu.VMEM((NY, 5, 8, 128), F32),
+            pltpu.VMEM((NZ, 2, 8, 128), F32),
             pltpu.VMEM((8, 8, 128), F32),
             pltpu.VMEM((NY, 8, 128), F32),
             pltpu.VMEM((NZ, 8, 128), F32),
@@ -477,7 +499,7 @@
             pltpu.VMEM((2, 4, NCH, 2, ROWS, CH), BF),
             pltpu.VMEM((NCH, ROWS, CH), F32),
             pltpu.VMEM((2, NCH, ROWS, CH), F32),
-            pltpu.SemaphoreType.DMA((20,)),
+            pltpu.SemaphoreType.DMA((10 + 2 * NCH,)),
             pltpu.SemaphoreType.DMA((NSEM,)),
             pltpu.SemaphoreType.DMA((NSEM,)),
         ],

time: 80.3 us -> 77.7 us (0.968)
  Pallas kernels: 79.5 us -> 76.9 us
    pallas_call x1, Pallas kernels: 77.6 us -> 75 us  [body(): pl.pallas_call(functools.partial(kernel, 0.15 / math.sqrt(width)), out_sh...]
where the time goes in v3:
time: 77.7 us; the launch traced here: 77.6 us
  Pallas kernels  76.9 us (99%)
    pallas_call x1, Pallas kernels, body(): pl.pallas_call(functools.partial(kernel, 0.15 / math.sqrt(width)), out_sh...  75 us
    pallas_call x1, Pallas kernels, body(): pl.pallas_call(hand_over, out_shape=(jax.ShapeDtypeStruct((8, 64), F32),...  1.91 us

profile of v3, /device:TPU:1, one launch (start us, length us, event | category | flops | bytes accessed | tf_op | source)
XLA Modules:
  0.0 77.6 jit_solution(5433382232985241543)
XLA Ops:
  0.6 75.0 %shard_map.95 = (f32[8,64]{1,0:T(8,128)}, f32[56,2560]{1,0:T(8,128)}) custom-call(bf16[256,1792]{1,0:T(8,128)(2,1)} %h_in.1, bf16[256,2560]{1,0:T(8,128)(2,1)} %r_in.1, bf16[56,2560]{1,0:T(8,128)(2,1)} %w_in.1, f32[8,32]{1,0:T(8,128)} %bitcast.5, f32[1,32]{1,0:T(1,128)} %bitcast.6, s32[1,32]{1,0:T(1,128)} %bitcast.7, s32[1,32]{1,0:T(1,128)} %len_in.1, ...), custom_call_target="tpu_custom_call" | custom-call | tf_op jit(solution)/shard_map/pallas_call | solution.py:467
  75.7 1.9 %shard_map.96 = (f32[8,64]{1,0:T(8,128)}, f32[56,2560]{1,0:T(8,128)}) custom-call(f32[8,64]{1,0:T(8,128)} %get-tuple-element.6.lr_in, f32[56,2560]{1,0:T(8,128)} %get-tuple-element.7.g_in), custom_call_target="tpu_custom_call" | custom-call | tf_op jit(solution)/shard_map/pallas_call | solution.py:511

commit v4 on v3

--- a/solution.py
+++ b/solution.py
@@ -19,8 +19,8 @@
 PAIR = 2 * ROWS
 FB = ROWS * NZ
 FALL = 2 * FB
-CHUNKS = tuple((i * 256, 256) for i in range(5))
-CH = 256
+CHUNKS = ((0, 384), (384, 512), (896, 384))
+CH = 512
 NCH = len(CHUNKS)
 NSEM = 200
 

time: 77.7 us -> 76.5 us (0.985)
  Pallas kernels: 76.9 us -> 75.8 us
    pallas_call x1, Pallas kernels: 75 us -> 73.8 us  [body(): pl.pallas_call(functools.partial(kernel, 0.15 / math.sqrt(width)), out_sh...]
where the time goes in v4:
time: 76.5 us; the launch traced here: 76.4 us
  Pallas kernels  75.8 us (99%)
    pallas_call x1, Pallas kernels, body(): pl.pallas_call(functools.partial(kernel, 0.15 / math.sqrt(width)), out_sh...  73.8 us
    pallas_call x1, Pallas kernels, body(): pl.pallas_call(hand_over, out_shape=(jax.ShapeDtypeStruct((8, 64), F32),...  1.91 us

profile of v4, /device:TPU:1, one launch (start us, length us, event | category | flops | bytes accessed | tf_op | source)
XLA Modules:
  0.0 76.4 jit_solution(15571674383847782767)
XLA Ops:
  0.6 73.8 %shard_map.95 = (f32[8,64]{1,0:T(8,128)}, f32[56,2560]{1,0:T(8,128)}) custom-call(bf16[256,1792]{1,0:T(8,128)(2,1)} %h_in.1, bf16[256,2560]{1,0:T(8,128)(2,1)} %r_in.1, bf16[56,2560]{1,0:T(8,128)(2,1)} %w_in.1, f32[8,32]{1,0:T(8,128)} %bitcast.5, f32[1,32]{1,0:T(1,128)} %bitcast.6, s32[1,32]{1,0:T(1,128)} %bitcast.7, s32[1,32]{1,0:T(1,128)} %len_in.1, ...), custom_call_target="tpu_custom_call" | custom-call | tf_op jit(solution)/shard_map/pallas_call | solution.py:467
  74.5 1.9 %shard_map.96 = (f32[8,64]{1,0:T(8,128)}, f32[56,2560]{1,0:T(8,128)}) custom-call(f32[8,64]{1,0:T(8,128)} %get-tuple-element.6.lr_in, f32[56,2560]{1,0:T(8,128)} %get-tuple-element.7.g_in), custom_call_target="tpu_custom_call" | custom-call | tf_op jit(solution)/shard_map/pallas_call | solution.py:511
